TPU v7x, 256 devices: a whole 4x4x8 slice. The times are simulated.
256 devices in a mesh: query: 16 (over z, y_lo), db: 16 (over x, y_hi, core).
Axes of the slice: x: 4, y: 4 (y_hi: 2, y_lo: 2; y = y_hi * 2 + y_lo), z: 8, core: 2. Of those that a mesh axis runs over, the one named last changes fastest.
Arguments:
- noisy_images: float32 [16, 3, 128, 128], P('db', None, 'query'), may hold values from -6 to 6
- database: bfloat16 [432, 262144], P(None, 'db'), may hold values from -4 to 4
- picked_blocks: int32 [16, 4], P('db'), may hold values from 0 to 7, as said below
- alpha_now: float32 [16], replicated, may hold values from 0.15 to 0.35
- alpha_next: float32 [16], replicated, may hold values from 0.4 to 0.8
Outputs:
- next_images: float32 [16, 3, 128, 128], P('db', None, 'query')
Inputs may be any that keep to these rules, and one draw needn't show every extreme that they name: `picked_blocks`: each row names 4 different windows of the 8 stored on that shard.
All inputs are finite; a program needn't handle non-finite values.
Results may differ from a plain program's by a relative error of at most 0.00075.
Values may be sent and summed in bfloat16 or wider, within the bound.
A program may use at most 192 MiB of HBM per device.

v0:
```python
import jax
import jax.numpy as jnp
from jax import lax
from jax.sharding import PartitionSpec as P

BLOCK = 2048


def shifted(value, axis, by):
    count = lax.axis_size(axis)
    return lax.ppermute(value, axis, [(i, (i + by) % count) for i in range(count)])


def combined_all(value, axis, combine):
    everything = jax.tree.map(lambda part: lax.all_gather(part, axis), value)
    first = jax.tree.map(lambda part: part[0], everything)

    def lap(k, so_far):
        return combine(so_far, jax.tree.map(lambda part: part[k], everything))

    return lax.fori_loop(1, lax.axis_size(axis), lap, first)


def extract(pixels):
    height = pixels.shape[2] - 8
    across = pixels.shape[3] - 8
    slab_list = []
    for row_shift in range(12):
        for col_shift in range(12):
            slab_list.append(
                pixels[:, :, row_shift : row_shift + height : 4, col_shift : col_shift + across : 4]
            )
    stacked = jnp.stack(slab_list)
    stacked = stacked.reshape(12, 12, stacked.shape[1], 3, stacked.shape[3], stacked.shape[4])
    stacked = jnp.transpose(stacked, (3, 0, 1, 2, 4, 5))
    return stacked.reshape(432, -1)


def combine(first, second):
    top = jnp.maximum(first[0], second[0])
    factor_one = jnp.exp(first[0] - top)
    factor_two = jnp.exp(second[0] - top)
    totals = first[1] * factor_one + second[1] * factor_two
    numerator = first[2] * factor_one[None, :] + second[2] * factor_two[None, :]
    return (top, totals, numerator)


def on_device(noisy_images, database, picked_blocks, alpha_now, alpha_next):
    images_dev, channels, height, across = noisy_images.shape
    rounded = noisy_images.astype(jnp.bfloat16)
    below = shifted(rounded, "query", -1)
    extended = jnp.concatenate([rounded, below], axis=2)
    extended = jnp.concatenate([extended, extended[:, :, :, :8]], axis=3)
    per_image = height // 4 * (across // 4)
    gathered = lax.all_gather(extract(extended), "db", axis=1, tiled=True)
    count = gathered.shape[1]
    per_query = jnp.repeat(alpha_now, per_image)
    linear = jnp.sqrt(per_query) / (1.0 - per_query)
    quadratic = per_query / (2.0 * (1.0 - per_query))
    maxima = jnp.full((count,), -jnp.inf, jnp.float32)
    totals = jnp.zeros((count,), jnp.float32)
    numerator = jnp.zeros((432, count), jnp.float32)
    for slot in range(picked_blocks.shape[1]):
        offset = picked_blocks[0, slot] * BLOCK
        window = lax.dynamic_slice_in_dim(database, offset, BLOCK, 1)
        squares = jnp.sum(window.astype(jnp.float32) ** 2, axis=0)
        inner = lax.dot_general(
            gathered, window, (((0,), (0,)), ((), ())), preferred_element_type=jnp.float32
        )
        logits = linear[:, None] * inner - quadratic[:, None] * squares[None, :]
        new_max = jnp.maximum(maxima, jnp.max(logits, axis=1))
        rescale = jnp.exp(maxima - new_max)
        raw = jnp.exp(logits - new_max[:, None])
        totals = totals * rescale + jnp.sum(raw, axis=1)
        weighted = lax.dot_general(
            window,
            raw.astype(jnp.bfloat16),
            (((1,), (1,)), ((), ())),
            preferred_element_type=jnp.float32,
        )
        numerator = numerator * rescale[None, :] + weighted
        maxima = new_max
    per_device = images_dev * per_image
    maxima, totals, numerator = combined_all((maxima, totals, numerator), "db", combine)
    own_start = lax.axis_index("db") * per_device
    totals = lax.dynamic_slice_in_dim(totals, own_start, per_device, 0)
    numerator = lax.dynamic_slice_in_dim(numerator, own_start, per_device, 1)
    estimate = numerator / totals[None, :]
    pieces = estimate.reshape(3, 3, 4, 3, 4, images_dev, height // 4, across // 4)
    accum = jnp.zeros((images_dev, 3, height // 4 + 2, 4, across // 4 + 2, 4), jnp.float32)
    for coarse_row in range(3):
        for coarse_col in range(3):
            piece = jnp.transpose(pieces[:, coarse_row, :, coarse_col], (3, 0, 4, 1, 5, 2))
            accum = accum + jnp.pad(
                piece,
                (
                    (0, 0),
                    (0, 0),
                    (coarse_row, 2 - coarse_row),
                    (0, 0),
                    (coarse_col, 2 - coarse_col),
                    (0, 0),
                ),
            )
    summed = accum.reshape(images_dev, 3, height + 8, across + 8)
    summed = summed[:, :, :, :across].at[:, :, :, :8].add(summed[:, :, :, across:])
    spill = shifted(summed[:, :, height:, :], "query", 1)
    denoised = summed[:, :, :height, :].at[:, :, :8, :].add(spill) / 9.0
    own_images = lax.axis_index("db") * images_dev
    signal = lax.dynamic_slice_in_dim(alpha_now, own_images, images_dev, 0)[:, None, None, None]
    after = lax.dynamic_slice_in_dim(alpha_next, own_images, images_dev, 0)[:, None, None, None]
    noise_part = (noisy_images - jnp.sqrt(signal) * denoised) / jnp.sqrt(1.0 - signal)
    return jnp.sqrt(after) * denoised + jnp.sqrt(1.0 - after) * noise_part


def solution(mesh):
    return jax.shard_map(
        on_device,
        mesh=mesh,
        in_specs=(P("db", None, "query", None), P(None, "db"), P("db", None), P(), P()),
        out_specs=P("db", None, "query", None),
        check_vma=False,
    )
```

profile of v0, /device:TPU:1, one launch (start us, length us, event | category | flops | bytes accessed | tf_op | source)
XLA Modules:
  0.0 337.6 jit_solution(15268145274604213155)
XLA Ops:
  7.2 7.4 %collective-permute-start = (bf16[1,3,8,128]{3,2,1,0:T(8,128)(2,1)S(1)}, bf16[1,3,8,128]{3,2,1,0:T(8,128)(2,1)S(1)}, u32[]{:S(2)}, u32[]{:S(2)}) collective-permute-start(bf16[1,3,8,128]{3,2,1,0:T(8,128)(2,1)S(1)} %convert_element_type.45), channel_id=1, source_target_pairs={{0,240},{16,0},{32,16},{48,32},{64,48},{80,64},{96,80},{112,96},{1... | collective-permute-start | bytes 18440 | tf_op jit(solution)/shard_map/ppermute | solution.py:11
  19.7 4.7 %multiply_reduce_fusion.2 = (f32[2048]{0:T(1024)S(1)}, f32[2048]{0:T(1024)S(1)}, f32[2048]{0:T(1024)S(1)}, f32[2048]{0:T(1024)S(1)}) fusion(bf16[432,16384]{1,0:T(8,128)(2,1)} %param.14, s32[]{:T(128)S(6)} %select_n.33, s32[]{:T(128)S(6)} %select_n.32, s32[]{:T(128)S(6)} %select_n.34, s32[]{:T(128)S(6)} %select_n.35), kind=kLoop, calls=%fused_computation.33 | loop fusion | flops 10608640 | bytes 7110672 | tf_op jit(solution)/shard_map/reduce_sum | solution.py:66
  45.1 27.8 %all_gather.17 = bf16[432,1024]{0,1:T(8,128)(2,1)S(1)} all-gather(bf16[432,64]{0,1:T(8,128)(2,1)S(1)} %copy.4668), channel_id=1, replica_groups=mesh['query'=16,'db'=16] {'db'}, dimensions={1}, use_global_device_ids=true | all-gather | bytes 940032 | tf_op jit(solution)/shard_map/all_gather | solution.py:55
  72.9 3.8 %fusion.24 = f32[1024,2048]{1,0:T(8,128)S(1)} fusion(bf16[432,1024]{0,1:T(8,128)(2,1)S(1)} %all_gather.17, bf16[432,16384]{1,0:T(8,128)(2,1)} %param.14, s32[]{:T(128)S(6)} %select_n.35), kind=kOutput, calls=%fused_computation.37 | convolution fusion | flops 1811939328 | bytes 11042820 | tf_op jit(solution)/shard_map/dot_general | solution.py:67
  76.8 8.5 %fusion.27 = f32[1024,2048]{1,0:T(8,128)} fusion(bf16[432,1024]{0,1:T(8,128)(2,1)S(1)} %all_gather.17, bf16[432,16384]{1,0:T(8,128)(2,1)} %param.14, s32[]{:T(128)S(6)} %select_n.34), kind=kOutput, calls=%fused_computation.40 | convolution fusion | flops 1811939328 | bytes 11042820 | tf_op jit(solution)/shard_map/dot_general | solution.py:67
  85.2 6.5 %fusion.9 = (f32[1024]{0:T(1024)S(1)}, f32[1024,2048]{1,0:T(8,128)}) fusion(f32[2048]{0:T(1024)S(1)} %get-tuple-element.217, f32[1024]{0:T(1024)S(1)} %get-tuple-element.266, f32[1024]{0:T(1024)S(1)} %get-tuple-element.265, bf16[432,1024]{0,1:T(8,128)(2,1)S(1)} %all_gather.17, bf16[432,16384]{1,0:T(8,128)(2,1)} %param.14, s32[]{:T(128)S(6)} %select_n.32), kind=kOutput, calls=%fused_computation.23 | convolution fusion | flops 1820326912 | bytes 11063300 | tf_op jit(solution)/shard_map/dot_general | solution.py:67
  91.7 12.9 %fusion.2 = (f32[1024]{0:T(1024)S(1)}, f32[1024]{0:T(1024)S(1)}, f32[1024]{0:T(1024)S(1)}, f32[1024]{0:T(1024)S(1)}, f32[1024,2048]{1,0:T(8,128)}) fusion(f32[1024,2048]{1,0:T(8,128)} %get-tuple-element.272, f32[1024]{0:T(1024)S(1)} %get-tuple-element.271, f32[2048]{0:T(1024)S(1)} %get-tuple-element.217, f32[1024]{0:T(1024)S(1)} %get-tuple-element.266, ...), kind=kOutput, calls=%fused_computation.16 | convolution fusion | flops 1847586816 | bytes 36270084 | tf_op jit(solution)/shard_map/dot_general | solution.py:67
  104.7 5.8 %fusion.15 = f32[432,1024]{1,0:T(8,128)S(1)} fusion(f32[1024,2048]{1,0:T(8,128)} %fusion.27, f32[1024]{0:T(1024)S(1)} %get-tuple-element.248, f32[2048]{0:T(1024)S(1)} %get-tuple-element.218, f32[1024]{0:T(1024)S(1)} %get-tuple-element.266, f32[1024]{0:T(1024)S(1)} %get-tuple-element.265, bf16[432,16384]{1,0:T(8,128)(2,1)} %param.14, s32[]{:T(128)S(6)} %select_n.34), kind=kOutput, calls=%fused_computation.28 | convolution fusion | flops 1822425088 | bytes 11948036 | tf_op jit(solution)/shard_map/dot_general | solution.py:75
  110.6 4.3 %fusion.13 = f32[432,1024]{1,0:T(8,128)S(1)} fusion(f32[1024,2048]{1,0:T(8,128)S(1)} %fusion.24, f32[1024]{0:T(1024)S(1)} %get-tuple-element.250, f32[2048]{0:T(1024)S(1)} %get-tuple-element.219, f32[1024]{0:T(1024)S(1)} %get-tuple-element.266, f32[1024]{0:T(1024)S(1)} %get-tuple-element.265, bf16[432,16384]{1,0:T(8,128)(2,1)} %param.14, s32[]{:T(128)S(6)} %select_n.35), kind=kOutput, calls=%fused_computation.27 | convolution fusion | flops 1822425088 | bytes 11948036 | tf_op jit(solution)/shard_map/dot_general | solution.py:75
  115.0 4.3 %fusion.17 = f32[432,1024]{1,0:T(8,128)S(1)} fusion(f32[1024,2048]{1,0:T(8,128)S(1)} %bitcast.375, f32[1024]{0:T(1024)S(1)} %get-tuple-element.246, f32[2048]{0:T(1024)S(1)} %get-tuple-element.216, f32[1024]{0:T(1024)S(1)} %get-tuple-element.266, f32[1024]{0:T(1024)S(1)} %get-tuple-element.265, bf16[432,16384]{1,0:T(8,128)(2,1)} %param.14, s32[]{:T(128)S(6)} %select_n.33), kind=kOutput, calls=%fused_computation.29 | convolution fusion | flops 1822425088 | bytes 11948036 | tf_op jit(solution)/shard_map/dot_general | solution.py:75
  119.3 6.3 %multiply_add_fusion.1 = f32[432,1024]{1,0:T(8,128)} fusion(f32[432,1024]{1,0:T(8,128)S(1)} %fusion.13, f32[432,1024]{1,0:T(8,128)S(1)} %fusion.15, f32[432,1024]{1,0:T(8,128)S(1)} %fusion.17, f32[1024,2048]{1,0:T(8,128)S(1)} %bitcast.393, f32[1024]{0:T(1024)S(1)} %get-tuple-element.271, f32[2048]{0:T(1024)S(1)} %get-tuple-element.217, ...), kind=kOutput, calls=%fused_computation.35 | convolution fusion | flops 1825521664 | bytes 17272836 | tf_op jit(solution)/shard_map/dot_general | solution.py:75
  125.7 12.2 %fusion.4 = (f32[1024]{0:T(1024)S(1)}, f32[1024]{0:T(1024)S(1)}, f32[1024]{0:T(1024)S(1)}) fusion(f32[1024,2048]{1,0:T(8,128)} %get-tuple-element.273, f32[1024]{0:T(1024)S(1)} %get-tuple-element.246, f32[2048]{0:T(1024)S(1)} %get-tuple-element.216, f32[1024]{0:T(1024)S(1)} %get-tuple-element.266, f32[1024]{0:T(1024)S(1)} %get-tuple-element.265, ...), kind=kLoop, calls=%fused_computation.18 | loop fusion | flops 31454208 | bytes 25223168 | tf_op jit(solution)/shard_map/reduce_sum | solution.py:74
  137.9 20.0 %all-gather.2 = f32[16,1,1024]{2,1,0:T(1,128)S(1)} all-gather(f32[1,1,1024]{2,1,0:T(1,128)S(1)} %get-tuple-element.262), channel_id=1, replica_groups=mesh['query'=16,'db'=16] {'db'}, dimensions={0}, use_global_device_ids=true | all-gather | bytes 69632 | tf_op jit(solution)/shard_map/all_gather | solution.py:15
  157.9 22.7 %all-gather.1 = f32[16,1,1024]{2,1,0:T(1,128)S(1)} all-gather(f32[1,1,1024]{2,1,0:T(1,128)S(1)} %get-tuple-element.263), channel_id=1, replica_groups=mesh['query'=16,'db'=16] {'db'}, dimensions={0}, use_global_device_ids=true | all-gather | bytes 69632 | tf_op jit(solution)/shard_map/all_gather | solution.py:15
  180.6 106.3 %all-gather.5.cloned.1.call-done = f32[6912,1024]{1,0:T(8,128)} async-done(((f32[432,1024]{1,0:T(8,128)}), f32[6912,1024]{1,0:T(8,128)}) %all-gather.5.cloned.1.call-update) | async-done | bytes 28311568 | tf_op jit(solution)/shard_map/all_gather | solution.py:15
  286.9 1.6 slice.722
  288.5 34.9 %while.22 = (s32[]{:T(128)}, f32[1024]{0:T(1024)S(1)}, f32[1024]{0:T(1024)S(1)}, f32[432,1024]{1,0:T(8,128)S(1)}, f32[16,1024]{1,0:T(8,128)S(1)}, /*index=5*/f32...) while((s32[]{:T(128)}, f32[1024]{0:T(1024)S(1)}, f32[1024]{0:T(1024)S(1)}, ...), condition=%wide.region_13.0_spmd, body=%wide.region_12.0_spmd.sunk | while | flops 1333253 | bytes 5365903 | solution.py:21
  288.6 2.3 fusion.50
  290.9 2.3 fusion.50
  293.2 2.3 fusion.50
  295.6 2.3 fusion.50
  297.9 2.3 fusion.50
  300.2 2.3 fusion.50
  302.5 2.3 fusion.50
  304.9 2.3 fusion.50
  307.2 2.3 fusion.50
  309.5 2.3 fusion.50
  311.9 2.3 fusion.50
  314.2 2.3 fusion.50
  316.5 2.3 fusion.50
  318.8 2.3 fusion.50
  321.2 2.3 fusion.50
  (374 shorter events, 28.5 us)
Async XLA Ops:
  6.5 280.3 %all-gather.5.cloned.1.call-start = ((), (), s32[]{:S(2)}) async-start(), calls=%async_computation | async-start | bytes 30081024 | tf_op jit(solution)/shard_map/all_gather | solution.py:15
  7.2 17.1 %collective-permute-start = (bf16[1,3,8,128]{3,2,1,0:T(8,128)(2,1)S(1)}, bf16[1,3,8,128]{3,2,1,0:T(8,128)(2,1)S(1)}, u32[]{:S(2)}, u32[]{:S(2)}) collective-permute-start(bf16[1,3,8,128]{3,2,1,0:T(8,128)(2,1)S(1)} %convert_element_type.45), channel_id=1, source_target_pairs={{0,240},{16,0},{32,16},{48,32},{64,48},{80,64},{96,80},{112,96},{1... | collective-permute-start | bytes 18440 | tf_op jit(solution)/shard_map/ppermute | solution.py:11
  76.7 33.8 %copy-start = (f32[1024,2048]{1,0:T(8,128)}, f32[1024,2048]{1,0:T(8,128)S(1)}, u32[]{:S(2)}) copy-start(f32[1024,2048]{1,0:T(8,128)S(1)} %fusion.24) | copy-start | bytes 25165828
  104.7 10.2 %slice-start = ((s8[8388608]{0:T(1024)(128)(4,1)}), s8[4194304]{0:T(1024)(128)(4,1)S(1)}, s32[]{:S(2)}) async-start(s8[8388608]{0:T(1024)(128)(4,1)} %bitcast.374), calls=%async_computation.1 | async-start | bytes 8388608
  110.6 4.4 %slice-start.1 = ((s8[8388608]{0:T(1024)(128)(4,1)}), s8[4194304]{0:T(1024)(128)(4,1)S(1)}, s32[]{:S(2)}) async-start(s8[8388608]{0:T(1024)(128)(4,1)} %bitcast.374), calls=%async_computation.2 | async-start | bytes 8388608
  110.6 8.7 %slice-start.2 = ((s8[8388608]{0:T(1024)(128)(4,1)}), s8[4194304]{0:T(1024)(128)(4,1)S(1)}, s32[]{:S(2)}) async-start(s8[8388608]{0:T(1024)(128)(4,1)} %bitcast.392), calls=%async_computation.3 | async-start | bytes 8388608
  115.0 4.3 %slice-start.3 = ((s8[8388608]{0:T(1024)(128)(4,1)}), s8[4194304]{0:T(1024)(128)(4,1)S(1)}, s32[]{:S(2)}) async-start(s8[8388608]{0:T(1024)(128)(4,1)} %bitcast.392), calls=%async_computation.4 | async-start | bytes 8388608
  288.5 37.3 %copy-start.2 = (f32[16]{0:T(128)S(1)}, f32[16]{0:T(128)}, u32[]{:S(2)}) copy-start(f32[16]{0:T(128)} %param.16) | copy-start | bytes 196
  288.5 39.2 %copy-start.3 = (f32[16]{0:T(128)S(1)}, f32[16]{0:T(128)}, u32[]{:S(2)}) copy-start(f32[16]{0:T(128)} %param.17) | copy-start | bytes 196
  288.5 41.7 %copy-start.1 = (f32[1,3,8,128]{3,2,1,0:T(8,128)S(1)}, f32[1,3,8,128]{3,2,1,0:T(8,128)}, u32[]{:S(2)}) copy-start(f32[1,3,8,128]{3,2,1,0:T(8,128)} %param.13) | copy-start | bytes 36868
  325.4 4.7 %collective-permute-start.1 = (f32[1,3,8,128]{3,2,1,0:T(8,128)S(1)}, f32[1,3,8,128]{3,2,1,0:T(8,128)S(1)}, u32[]{:S(2)}, u32[]{:S(2)}) collective-permute-start(f32[1,3,8,128]{3,2,1,0:T(8,128)S(1)} %slice.736), channel_id=1, source_target_pairs={{0,16},{16,32},{32,48},{48,64},{64,80},{80,96},{96,112},{112,128},... | collective-permute-start | bytes 36872 | tf_op jit(solution)/shard_map/ppermute | solution.py:11
Sparse Core Ops, SparseCore 0:
  125.8 161.0 all-gather.4
where the time goes:
time: 338 us
  waiting for transfers between devices  107 us (32%)
  blocking collectives  70.5 us (21%)
  other arithmetic  53 us (16%)
  matrix products  52.5 us (16%)
  local copies, waits for them, and re-layouts  27.1 us (8%)
  between operations  19.5 us (6%)
  starting transfers between devices  7.79 us (2%)
    all_gather x1, waiting for transfers between devices, combined_all(): everything = jax.tree.map(lambda part: lax.all_gather(part, axis), value)  106 us
    all_gather x2, blocking collectives, combined_all(): everything = jax.tree.map(lambda part: lax.all_gather(part, axis), value)  42.7 us
    add x15, other arithmetic, combine(): numerator = first[2] * factor_one[None, :] + second[2] * factor_two[None, :]  34 us
    dot_general x4, matrix products, on_device(): lax.dot_general(gathered, window, (((0,), (0,)), ((), ())), preferred_ele...  31.7 us
    all_gather x1, blocking collectives, on_device(): gathered = lax.all_gather(extract(extended), 'db', axis=1, tiled=True)  27.8 us
    dot_general x4, matrix products, on_device(): lax.dot_general(window, raw.astype(jnp.bfloat16), (((1,), (1,)), ((), ())...  20.8 us
    slice x144, local copies, waits for them, and re-layouts, extract(): pixels[:, :, row_shift:row_shift + height:4, col_shift:col_shift + across:4]  18.4 us
    reduce_sum x1, other arithmetic, on_device(): totals = totals * rescale + jnp.sum(raw, axis=1)  12.2 us
  transfers between devices with their start and end apart: 3, of which 2 were waited for; matrix products, arithmetic and copies ran while one was open for 6% of the time, Pallas kernels for 0%

commit v1 on v0

--- a/solution.py
+++ b/solution.py
@@ -52,7 +52,9 @@
     extended = jnp.concatenate([rounded, below], axis=2)
     extended = jnp.concatenate([extended, extended[:, :, :, :8]], axis=3)
     per_image = height // 4 * (across // 4)
-    gathered = lax.all_gather(extract(extended), "db", axis=1, tiled=True)
+    gathered = jnp.concatenate(
+        lax.all_to_all(jnp.stack([extract(extended)] * lax.axis_size("db")), "db", 0, 0), axis=1
+    )
     count = gathered.shape[1]
     per_query = jnp.repeat(alpha_now, per_image)
     linear = jnp.sqrt(per_query) / (1.0 - per_query)

time: 338 us -> 332 us (0.982)
  blocking collectives: 70.5 us -> 44.1 us
  waiting for transfers between devices: 107 us -> 118 us
  starting transfers between devices: 7.79 us -> 16.2 us
    all_gather x1 -> x0, blocking collectives: 27.8 us -> none  [on_device(): gathered = lax.all_gather(extract(extended), 'db', axis=1, tiled=True)]
    all_to_all x0 -> x1, starting transfers between devices: none -> 8.36 us  [on_device(): lax.all_to_all(jnp.stack([extract(extended)] * lax.axis_size('db')), 'db'...]
    all_to_all x0 -> x1, waiting for transfers between devices: none -> 7.34 us  [on_device(): lax.all_to_all(jnp.stack([extract(extended)] * lax.axis_size('db')), 'db'...]
  transfers between devices with their start and end apart: 3 -> 4, of which waited for: 2 -> 4; matrix products, arithmetic and copies ran while one was open for 6% -> 6% of each run, Pallas kernels for 0% -> 0%
where the time goes in v1:
time: 332 us; the launch traced here: 331 us
  waiting for transfers between devices  118 us (36%)
  matrix products  52.4 us (16%)
  other arithmetic  52.2 us (16%)
  blocking collectives  44.1 us (13%)
  local copies, waits for them, and re-layouts  28.1 us (8%)
  between operations  19.5 us (6%)
  starting transfers between devices  16.2 us (5%)
    all_gather x1, waiting for transfers between devices, combined_all(): everything = jax.tree.map(lambda part: lax.all_gather(part, axis), value)  109 us
    all_gather x2, blocking collectives, combined_all(): everything = jax.tree.map(lambda part: lax.all_gather(part, axis), value)  44.1 us
    add x15, other arithmetic, combine(): numerator = first[2] * factor_one[None, :] + second[2] * factor_two[None, :]  34 us
    dot_general x4, matrix products, on_device(): lax.dot_general(gathered, window, (((0,), (0,)), ((), ())), preferred_ele...  31.6 us
    dot_general x4, matrix products, on_device(): lax.dot_general(window, raw.astype(jnp.bfloat16), (((1,), (1,)), ((), ())...  20.8 us
    slice x144, local copies, waits for them, and re-layouts, extract(): pixels[:, :, row_shift:row_shift + height:4, col_shift:col_shift + across:4]  18.2 us
    reduce_sum x1, other arithmetic, on_device(): totals = totals * rescale + jnp.sum(raw, axis=1)  11.5 us
    all_to_all x1, starting transfers between devices, on_device(): lax.all_to_all(jnp.stack([extract(extended)] * lax.axis_size('db')), 'db'...  8.36 us
  transfers between devices with their start and end apart: 4, of which 4 were waited for; matrix products, arithmetic and copies ran while one was open for 6% of the time, Pallas kernels for 0%

profile of v1, /device:TPU:1, one launch (start us, length us, event | category | flops | bytes accessed | tf_op | source)
XLA Modules:
  0.0 330.7 jit_solution(5302857340418467439)
XLA Ops:
  7.2 7.4 %collective-permute-start = (bf16[1,3,8,128]{3,2,1,0:T(8,128)(2,1)S(1)}, bf16[1,3,8,128]{3,2,1,0:T(8,128)(2,1)S(1)}, u32[]{:S(2)}, u32[]{:S(2)}) collective-permute-start(bf16[1,3,8,128]{3,2,1,0:T(8,128)(2,1)S(1)} %convert_element_type.45), channel_id=1, source_target_pairs={{0,240},{16,0},{32,16},{48,32},{64,48},{80,64},{96,80},{112,96},{1... | collective-permute-start | bytes 18440 | tf_op jit(solution)/shard_map/ppermute | solution.py:11
  37.1 8.4 %all-to-all-start = ((bf16[16,432,64]{1,2,0:T(8,128)(2,1)}), bf16[16,432,64]{1,2,0:T(8,128)(2,1)S(1)}, u32[]{:S(2)}, u32[]{:S(2)}) async-start(bf16[16,432,64]{1,2,0:T(8,128)(2,1)} %stack.583), calls=%async_computation | async-start | bytes 2097152 | tf_op jit(solution)/shard_map/all_to_all | solution.py:56
  50.4 4.7 %multiply_reduce_fusion.2 = (f32[2048]{0:T(1024)S(1)}, f32[2048]{0:T(1024)S(1)}, f32[2048]{0:T(1024)S(1)}, f32[2048]{0:T(1024)S(1)}) fusion(bf16[432,16384]{1,0:T(8,128)(2,1)} %param.14, s32[]{:T(128)S(6)} %select_n.33, s32[]{:T(128)S(6)} %select_n.32, s32[]{:T(128)S(6)} %select_n.34, s32[]{:T(128)S(6)} %select_n.35), kind=kLoop, calls=%fused_computation.33 | loop fusion | flops 10608640 | bytes 7110672 | tf_op jit(solution)/shard_map/reduce_sum | solution.py:68
  55.1 7.3 %all-to-all-done = bf16[16,432,64]{1,2,0:T(8,128)(2,1)S(1)} async-done(((bf16[16,432,64]{1,2,0:T(8,128)(2,1)}), bf16[16,432,64]{1,2,0:T(8,128)(2,1)S(1)}, u32[]{:S(2)}, u32[]{:S(2)}) %all-to-all-start) | async-done | bytes 884768 | tf_op jit(solution)/shard_map/all_to_all | solution.py:56
  62.4 3.8 %fusion.24 = f32[1024,2048]{1,0:T(8,128)S(1)} fusion(bf16[432,1024]{0,1:T(8,128)(2,1)S(1)} %bitcast.380, bf16[432,16384]{1,0:T(8,128)(2,1)} %param.14, s32[]{:T(128)S(6)} %select_n.35), kind=kOutput, calls=%fused_computation.37 | convolution fusion | flops 1811939328 | bytes 11042820 | tf_op jit(solution)/shard_map/dot_general | solution.py:69
  66.2 8.5 %fusion.27 = f32[1024,2048]{1,0:T(8,128)} fusion(bf16[432,1024]{0,1:T(8,128)(2,1)S(1)} %bitcast.381, bf16[432,16384]{1,0:T(8,128)(2,1)} %param.14, s32[]{:T(128)S(6)} %select_n.34), kind=kOutput, calls=%fused_computation.40 | convolution fusion | flops 1811939328 | bytes 11042820 | tf_op jit(solution)/shard_map/dot_general | solution.py:69
  74.7 6.4 %fusion.9 = (f32[1024]{0:T(1024)S(1)}, f32[1024,2048]{1,0:T(8,128)}) fusion(f32[2048]{0:T(1024)S(1)} %get-tuple-element.217, f32[1024]{0:T(1024)S(1)} %get-tuple-element.266, f32[1024]{0:T(1024)S(1)} %get-tuple-element.265, bf16[432,1024]{0,1:T(8,128)(2,1)S(1)} %bitcast.382, bf16[432,16384]{1,0:T(8,128)(2,1)} %param.14, s32[]{:T(128)S(6)} %select_n.32), kind=kOutput, calls=%fused_computation.23 | convolution fusion | flops 1820326912 | bytes 11063300 | tf_op jit(solution)/shard_map/dot_general | solution.py:69
  81.1 12.9 %fusion.2 = (f32[1024]{0:T(1024)S(1)}, f32[1024]{0:T(1024)S(1)}, f32[1024]{0:T(1024)S(1)}, f32[1024]{0:T(1024)S(1)}, f32[1024,2048]{1,0:T(8,128)}) fusion(f32[1024,2048]{1,0:T(8,128)} %get-tuple-element.272, f32[1024]{0:T(1024)S(1)} %get-tuple-element.271, f32[2048]{0:T(1024)S(1)} %get-tuple-element.217, f32[1024]{0:T(1024)S(1)} %get-tuple-element.266, ...), kind=kOutput, calls=%fused_computation.16 | convolution fusion | flops 1847586816 | bytes 36270084 | tf_op jit(solution)/shard_map/dot_general | solution.py:69
  94.0 5.8 %fusion.15 = f32[432,1024]{1,0:T(8,128)S(1)} fusion(f32[1024,2048]{1,0:T(8,128)} %fusion.27, f32[1024]{0:T(1024)S(1)} %get-tuple-element.248, f32[2048]{0:T(1024)S(1)} %get-tuple-element.218, f32[1024]{0:T(1024)S(1)} %get-tuple-element.266, f32[1024]{0:T(1024)S(1)} %get-tuple-element.265, bf16[432,16384]{1,0:T(8,128)(2,1)} %param.14, s32[]{:T(128)S(6)} %select_n.34), kind=kOutput, calls=%fused_computation.28 | convolution fusion | flops 1822425088 | bytes 11948036 | tf_op jit(solution)/shard_map/dot_general | solution.py:77
  99.9 4.3 %fusion.13 = f32[432,1024]{1,0:T(8,128)S(1)} fusion(f32[1024,2048]{1,0:T(8,128)S(1)} %fusion.24, f32[1024]{0:T(1024)S(1)} %get-tuple-element.250, f32[2048]{0:T(1024)S(1)} %get-tuple-element.219, f32[1024]{0:T(1024)S(1)} %get-tuple-element.266, f32[1024]{0:T(1024)S(1)} %get-tuple-element.265, bf16[432,16384]{1,0:T(8,128)(2,1)} %param.14, s32[]{:T(128)S(6)} %select_n.35), kind=kOutput, calls=%fused_computation.27 | convolution fusion | flops 1822425088 | bytes 11948036 | tf_op jit(solution)/shard_map/dot_general | solution.py:77
  104.3 4.3 %fusion.17 = f32[432,1024]{1,0:T(8,128)S(1)} fusion(f32[1024,2048]{1,0:T(8,128)S(1)} %bitcast.378, f32[1024]{0:T(1024)S(1)} %get-tuple-element.246, f32[2048]{0:T(1024)S(1)} %get-tuple-element.216, f32[1024]{0:T(1024)S(1)} %get-tuple-element.266, f32[1024]{0:T(1024)S(1)} %get-tuple-element.265, bf16[432,16384]{1,0:T(8,128)(2,1)} %param.14, s32[]{:T(128)S(6)} %select_n.33), kind=kOutput, calls=%fused_computation.29 | convolution fusion | flops 1822425088 | bytes 11948036 | tf_op jit(solution)/shard_map/dot_general | solution.py:77
  108.6 6.3 %multiply_add_fusion.1 = f32[432,1024]{1,0:T(8,128)} fusion(f32[432,1024]{1,0:T(8,128)S(1)} %fusion.13, f32[432,1024]{1,0:T(8,128)S(1)} %fusion.15, f32[432,1024]{1,0:T(8,128)S(1)} %fusion.17, f32[1024,2048]{1,0:T(8,128)S(1)} %bitcast.400, f32[1024]{0:T(1024)S(1)} %get-tuple-element.271, f32[2048]{0:T(1024)S(1)} %get-tuple-element.217, ...), kind=kOutput, calls=%fused_computation.35 | convolution fusion | flops 1825521664 | bytes 17272836 | tf_op jit(solution)/shard_map/dot_general | solution.py:77
  115.0 11.5 %fusion.4 = (f32[1024]{0:T(1024)S(1)}, f32[1024]{0:T(1024)S(1)}, f32[1024]{0:T(1024)S(1)}) fusion(f32[1024,2048]{1,0:T(8,128)} %get-tuple-element.273, f32[1024]{0:T(1024)S(1)} %get-tuple-element.246, f32[2048]{0:T(1024)S(1)} %get-tuple-element.216, f32[1024]{0:T(1024)S(1)} %get-tuple-element.266, f32[1024]{0:T(1024)S(1)} %get-tuple-element.265, ...), kind=kLoop, calls=%fused_computation.18 | loop fusion | flops 31454208 | bytes 25223168 | tf_op jit(solution)/shard_map/reduce_sum | solution.py:76
  126.5 21.0 %all-gather.2 = f32[16,1,1024]{2,1,0:T(1,128)S(1)} all-gather(f32[1,1,1024]{2,1,0:T(1,128)S(1)} %get-tuple-element.262), channel_id=1, replica_groups=mesh['query'=16,'db'=16] {'db'}, dimensions={0}, use_global_device_ids=true | all-gather | bytes 69632 | tf_op jit(solution)/shard_map/all_gather | solution.py:15
  147.5 23.1 %all-gather.1 = f32[16,1,1024]{2,1,0:T(1,128)S(1)} all-gather(f32[1,1,1024]{2,1,0:T(1,128)S(1)} %get-tuple-element.263), channel_id=1, replica_groups=mesh['query'=16,'db'=16] {'db'}, dimensions={0}, use_global_device_ids=true | all-gather | bytes 69632 | tf_op jit(solution)/shard_map/all_gather | solution.py:15
  170.6 109.4 %all-gather.5.cloned.1.call-done = f32[6912,1024]{1,0:T(8,128)} async-done(((f32[432,1024]{1,0:T(8,128)}), f32[6912,1024]{1,0:T(8,128)}) %all-gather.5.cloned.1.call-update) | async-done | bytes 28311568 | tf_op jit(solution)/shard_map/all_gather | solution.py:15
  281.6 34.9 %while.22 = (s32[]{:T(128)}, f32[1024]{0:T(1024)S(1)}, f32[1024]{0:T(1024)S(1)}, f32[432,1024]{1,0:T(8,128)S(1)}, f32[16,1024]{1,0:T(8,128)S(1)}, /*index=5*/f32...) while((s32[]{:T(128)}, f32[1024]{0:T(1024)S(1)}, f32[1024]{0:T(1024)S(1)}, ...), condition=%wide.region_13.0_spmd, body=%wide.region_12.0_spmd.sunk | while | flops 1333253 | bytes 5365903 | solution.py:21
  281.7 2.3 fusion.50
  284.0 2.3 fusion.50
  286.3 2.3 fusion.50
  288.7 2.3 fusion.50
  291.0 2.3 fusion.50
  293.3 2.3 fusion.50
  295.7 2.3 fusion.50
  298.0 2.3 fusion.50
  300.3 2.3 fusion.50
  302.7 2.3 fusion.50
  305.0 2.3 fusion.50
  307.3 2.3 fusion.50
  309.6 2.3 fusion.50
  312.0 2.3 fusion.50
  314.3 2.3 fusion.50
  (376 shorter events, 31.7 us)
Async XLA Ops:
  7.2 8.2 %collective-permute-start = (bf16[1,3,8,128]{3,2,1,0:T(8,128)(2,1)S(1)}, bf16[1,3,8,128]{3,2,1,0:T(8,128)(2,1)S(1)}, u32[]{:S(2)}, u32[]{:S(2)}) collective-permute-start(bf16[1,3,8,128]{3,2,1,0:T(8,128)(2,1)S(1)} %convert_element_type.45), channel_id=1, source_target_pairs={{0,240},{16,0},{32,16},{48,32},{64,48},{80,64},{96,80},{112,96},{1... | collective-permute-start | bytes 18440 | tf_op jit(solution)/shard_map/ppermute | solution.py:11
  37.1 25.3 %all-to-all-start = ((bf16[16,432,64]{1,2,0:T(8,128)(2,1)}), bf16[16,432,64]{1,2,0:T(8,128)(2,1)S(1)}, u32[]{:S(2)}, u32[]{:S(2)}) async-start(bf16[16,432,64]{1,2,0:T(8,128)(2,1)} %stack.583), calls=%async_computation | async-start | bytes 2097152 | tf_op jit(solution)/shard_map/all_to_all | solution.py:56
  45.5 234.5 %all-gather.5.cloned.1.call-start = ((), (), s32[]{:S(2)}) async-start(), calls=%async_computation.1 | async-start | bytes 30081024 | tf_op jit(solution)/shard_map/all_gather | solution.py:15
  66.2 33.7 %copy-start = (f32[1024,2048]{1,0:T(8,128)}, f32[1024,2048]{1,0:T(8,128)S(1)}, u32[]{:S(2)}) copy-start(f32[1024,2048]{1,0:T(8,128)S(1)} %fusion.24) | copy-start | bytes 25165828
  94.0 10.2 %slice-start = ((s8[8388608]{0:T(1024)(128)(4,1)}), s8[4194304]{0:T(1024)(128)(4,1)S(1)}, s32[]{:S(2)}) async-start(s8[8388608]{0:T(1024)(128)(4,1)} %bitcast.377), calls=%async_computation.2 | async-start | bytes 8388608
  99.9 4.4 %slice-start.1 = ((s8[8388608]{0:T(1024)(128)(4,1)}), s8[4194304]{0:T(1024)(128)(4,1)S(1)}, s32[]{:S(2)}) async-start(s8[8388608]{0:T(1024)(128)(4,1)} %bitcast.377), calls=%async_computation.3 | async-start | bytes 8388608
  99.9 8.7 %slice-start.2 = ((s8[8388608]{0:T(1024)(128)(4,1)}), s8[4194304]{0:T(1024)(128)(4,1)S(1)}, s32[]{:S(2)}) async-start(s8[8388608]{0:T(1024)(128)(4,1)} %bitcast.399), calls=%async_computation.4 | async-start | bytes 8388608
  104.3 4.3 %slice-start.3 = ((s8[8388608]{0:T(1024)(128)(4,1)}), s8[4194304]{0:T(1024)(128)(4,1)S(1)}, s32[]{:S(2)}) async-start(s8[8388608]{0:T(1024)(128)(4,1)} %bitcast.399), calls=%async_computation.5 | async-start | bytes 8388608
  281.6 37.3 %copy-start.2 = (f32[16]{0:T(128)S(1)}, f32[16]{0:T(128)}, u32[]{:S(2)}) copy-start(f32[16]{0:T(128)} %param.16) | copy-start | bytes 196
  281.6 39.2 %copy-start.3 = (f32[16]{0:T(128)S(1)}, f32[16]{0:T(128)}, u32[]{:S(2)}) copy-start(f32[16]{0:T(128)} %param.17) | copy-start | bytes 196
  281.6 41.7 %copy-start.1 = (f32[1,3,8,128]{3,2,1,0:T(8,128)S(1)}, f32[1,3,8,128]{3,2,1,0:T(8,128)}, u32[]{:S(2)}) copy-start(f32[1,3,8,128]{3,2,1,0:T(8,128)} %param.13) | copy-start | bytes 36868
  318.5 4.7 %collective-permute-start.1 = (f32[1,3,8,128]{3,2,1,0:T(8,128)S(1)}, f32[1,3,8,128]{3,2,1,0:T(8,128)S(1)}, u32[]{:S(2)}, u32[]{:S(2)}) collective-permute-start(f32[1,3,8,128]{3,2,1,0:T(8,128)S(1)} %slice.736), channel_id=1, source_target_pairs={{0,16},{16,32},{32,48},{48,64},{64,80},{80,96},{96,112},{112,128},... | collective-permute-start | bytes 36872 | tf_op jit(solution)/shard_map/ppermute | solution.py:11
Sparse Core Ops, SparseCore 0:
  115.1 164.8 all-gather.4
